TPU v7x, 512 devices: a whole 4x8x8 slice. The times are simulated.
512 devices in a mesh: row: 64 (over y_lo, z, x), col: 8 (over y_hi, core).
Axes of the slice: x: 4, y: 8 (y_hi: 4, y_lo: 2; y = y_hi * 2 + y_lo), z: 8, core: 2. Of those that a mesh axis runs over, the one named last changes fastest.
Arguments:
- orbitals: bfloat16 [16384, 2, 256], P(('row', 'col')), may hold values from -6 to 6
- kernel: bfloat16 [16384, 16384], P('row', 'col'), may hold values from -0.0029296875 to 0.0029296875
- basis: bfloat16 [16384, 2048], P('row'), may hold values from -0.046875 to 0.046875
Outputs:
- exchange: float32 [2048, 2, 256], P('row')
All inputs are finite; a program needn't handle non-finite values.
Results may differ from a plain program's by a relative error of at most 0.0041.
Values may be sent and summed in bfloat16 or wider, within the bound.
A program may use at most 64 MiB of HBM per device.

v0:
```python
import jax
import jax.numpy as jnp
from jax import lax
from jax.sharding import PartitionSpec as P


def body(orbitals, kernel, basis):
    row_orbitals = lax.all_gather(orbitals, "col", axis=0, tiled=True)
    point_rows = row_orbitals.shape[0]
    occupied = orbitals.shape[2]
    column_orbitals = lax.all_gather(orbitals, "row", axis=0, tiled=True)
    density = jnp.einsum(
        "psi,qsi->spq", row_orbitals, column_orbitals, preferred_element_type=jnp.float32
    )
    weighted = (density * kernel[None].astype(jnp.float32)).astype(jnp.bfloat16)
    applied = jnp.einsum(
        "spq,qsi->psi", weighted, column_orbitals, preferred_element_type=jnp.float32
    )
    out_rows = basis.shape[1] // lax.axis_size("row")
    summed = lax.psum(applied, "col").astype(jnp.bfloat16)
    flattened = summed.reshape(point_rows, -1)
    result = lax.psum_scatter(
        lax.dot_general(
            basis, flattened, (((0,), (0,)), ((), ())), preferred_element_type=jnp.float32
        ),
        "row",
        scatter_dimension=0,
        tiled=True,
    )
    return result.reshape(out_rows, 2, occupied)


def solution(mesh):
    return jax.shard_map(
        body,
        mesh=mesh,
        in_specs=(P(("row", "col"), None, None), P("row", "col"), P("row", None)),
        out_specs=P("row", None, None),
        check_vma=False,
    )
```

profile of v0, /device:TPU:40, one launch (start us, length us, event | category | flops | bytes accessed | tf_op | source)
XLA Modules:
  0.0 696.5 jit_solution(10531159770175762090)
XLA Ops:
  6.5 0.0 copy-start
  6.5 0.0 copy-start.1
  6.5 0.0 all-gather.2.cloned.1.call-start
  6.5 1.5 copy.9
  8.0 0.0 all-gather.2.cloned.1.call-update
  8.0 0.0 reduce-scatter.4.cloned.1.call-start
  8.1 1.5 convert_element_type.10
  9.6 0.0 copy-done.1
  9.6 14.6 %all_gather.6 = bf16[256,2,256]{2,1,0:T(2,128)(2,1)S(1)} all-gather(bf16[32,2,256]{2,1,0:T(2,128)(2,1)S(1)} %copy-done.1), channel_id=1, replica_groups=mesh['row'=64,'col'=8] {'col'}, dimensions={0}, use_global_device_ids=true | all-gather | bytes 294912 | tf_op jit(solution)/shard_map/all_gather | solution.py:8
  24.2 292.6 %all-gather.2.cloned.1.call-done = bf16[2048,2,256]{2,0,1:T(8,128)(2,1)} async-done(((bf16[32,2,256]{2,0,1:T(8,128)(2,1)}), bf16[2048,2,256]{2,0,1:T(8,128)(2,1)}) %all-gather.2.cloned.1.call-update) | async-done | bytes 2097168 | tf_op jit(solution)/shard_map/all_gather | solution.py:11
  316.8 4.3 fusion.1
  321.1 35.5 %all-reduce.1 = bf16[256,2,256]{2,0,1:T(8,128)(2,1)S(1)} all-reduce(f32[256,2,256]{2,0,1:T(8,128)} %fusion.1), channel_id=1, replica_groups=mesh['row'=64,'col'=8] {'col'}, use_global_device_ids=true, to_apply=%region_0.0 | all-reduce | flops 131072 | bytes 786432 | tf_op jit(solution)/shard_map/psum | solution.py:20
  356.6 0.1 copy.11
  356.7 0.0 copy-done
  356.7 2.7 convolution_bitcast_fusion
  359.4 5.3 copy.13
  364.8 0.0 reduce-scatter.4.cloned.1.call-update
  364.8 323.2 %reduce-scatter.4.cloned.1.call-done = f32[32,512]{1,0:T(8,128)} async-done(((f32[2048,512]{1,0:T(8,128)}), f32[32,512]{1,0:T(8,128)}) %reduce-scatter.4.cloned.1.call-update) | async-done | bytes 65552
  687.9 1.0 copy.14
  688.9 0.7 copy.12
Async XLA Ops:
  6.5 350.2 %copy-start = (bf16[256,2048]{1,0:T(8,128)(2,1)S(1)}, bf16[256,2048]{1,0:T(8,128)(2,1)}, u32[]{:S(2)}) copy-start(bf16[256,2048]{1,0:T(8,128)(2,1)} %param.5) | copy-start | bytes 3145732
  6.5 3.0 copy-start.1
  6.5 310.2 %all-gather.2.cloned.1.call-start = ((), (), s32[]{:S(2)}) async-start(), calls=%async_computation.1 | async-start | bytes 2129920 | tf_op jit(solution)/shard_map/all_gather | solution.py:11
  8.0 679.9 %reduce-scatter.4.cloned.1.call-start = ((), (), s32[]{:S(2)}) async-start(), calls=%async_computation.2 | async-start | bytes 4259840
Sparse Core Ops, SparseCore 0:
  9.4 307.2 all-gather.1
  364.9 322.9 reduce-scatter.3
where the time goes:
time: 697 us; the launch traced here: 696 us
  waiting for transfers between devices  616 us (88%)
  blocking collectives  50.1 us (7%)
  between operations  13.5 us (2%)
  local copies, waits for them, and re-layouts  8.66 us (1%)
  matrix products  6.99 us (1%)
    unnamed x3, waiting for transfers between devices  323 us
    all_gather x1, waiting for transfers between devices, body(): column_orbitals = lax.all_gather(orbitals, 'row', axis=0, tiled=True)  293 us
    psum x1, blocking collectives, body(): summed = lax.psum(applied, 'col').astype(jnp.bfloat16)  35.5 us
    all_gather x1, blocking collectives, body(): row_orbitals = lax.all_gather(orbitals, 'col', axis=0, tiled=True)  14.6 us
  transfers between devices with their start and end apart: 2, of which 2 were waited for; matrix products, arithmetic and copies ran while one was open for 0% of the time, Pallas kernels for 0%

commit v1 on v0

--- a/solution.py
+++ b/solution.py
@@ -8,7 +8,9 @@
     row_orbitals = lax.all_gather(orbitals, "col", axis=0, tiled=True)
     point_rows = row_orbitals.shape[0]
     occupied = orbitals.shape[2]
-    column_orbitals = lax.all_gather(orbitals, "row", axis=0, tiled=True)
+    column_orbitals = jnp.concatenate(
+        lax.all_to_all(jnp.stack([orbitals] * lax.axis_size("row")), "row", 0, 0), axis=0
+    )
     density = jnp.einsum(
         "psi,qsi->spq", row_orbitals, column_orbitals, preferred_element_type=jnp.float32
     )

time: 697 us -> 456 us (0.65)
  waiting for transfers between devices: 616 us -> 339 us
  blocking collectives: 50.1 us -> 67.4 us
  starting transfers between devices: 0.04 us -> 14.9 us
    all_gather x1 -> x0, waiting for transfers between devices: 293 us -> none  [body(): column_orbitals = lax.all_gather(orbitals, 'row', axis=0, tiled=True)]
    all_gather x1, blocking collectives: 14.6 us -> 32.7 us  [body(): row_orbitals = lax.all_gather(orbitals, 'col', axis=0, tiled=True)]
    all_to_all x0 -> x1, starting transfers between devices: none -> 14.9 us  [body(): lax.all_to_all(jnp.stack([orbitals] * lax.axis_size('row')), 'row', 0, 0)]
    all_to_all x0 -> x1, waiting for transfers between devices: none -> 13.5 us  [body(): lax.all_to_all(jnp.stack([orbitals] * lax.axis_size('row')), 'row', 0, 0)]
    unnamed x3 -> x2, waiting for transfers between devices: 323 us -> 326 us
  transfers between devices with their start and end apart: 2 -> 2, of which waited for: 2 -> 2; matrix products, arithmetic and copies ran while one was open for 0% -> 1% of each run, Pallas kernels for 0% -> 0%
where the time goes in v1:
time: 456 us
  waiting for transfers between devices  339 us (74%)
  blocking collectives  67.4 us (15%)
  starting transfers between devices  14.9 us (3%)
  between operations  13.5 us (3%)
  local copies, waits for them, and re-layouts  11.1 us (2%)
  matrix products  6.82 us (1%)
    unnamed x2, waiting for transfers between devices  326 us
    psum x1, blocking collectives, body(): summed = lax.psum(applied, 'col').astype(jnp.bfloat16)  34.7 us
    all_gather x1, blocking collectives, body(): row_orbitals = lax.all_gather(orbitals, 'col', axis=0, tiled=True)  32.7 us
    all_to_all x1, starting transfers between devices, body(): lax.all_to_all(jnp.stack([orbitals] * lax.axis_size('row')), 'row', 0, 0)  14.9 us
    all_to_all x1, waiting for transfers between devices, body(): lax.all_to_all(jnp.stack([orbitals] * lax.axis_size('row')), 'row', 0, 0)  13.5 us
  transfers between devices with their start and end apart: 2, of which 2 were waited for; matrix products, arithmetic and copies ran while one was open for 1% of the time, Pallas kernels for 0%

profile of v1, /device:TPU:40, one launch (start us, length us, event | category | flops | bytes accessed | tf_op | source)
XLA Modules:
  0.0 455.6 jit_solution(8143492601367600273)
XLA Ops:
  6.5 0.0 copy-start
  6.5 0.9 copy.9
  7.4 1.6 stack.2
  9.0 14.9 %all-to-all-start = ((bf16[64,32,2,256]{3,1,2,0:T(8,128)(2,1)}), bf16[64,32,2,256]{3,1,2,0:T(8,128)(2,1)S(1)}, u32[]{:S(2)}, u32[]{:S(2)}) async-start(bf16[64,32,2,256]{3,1,2,0:T(8,128)(2,1)} %stack.2), calls=%async_computation | async-start | bytes 4194304 | tf_op jit(solution)/shard_map/all_to_all | solution.py:12
  23.9 0.0 copy-start.1
  23.9 0.0 reduce-scatter.4.cloned.1.call-start
  23.9 2.8 convert_element_type.10
  26.7 0.0 copy-done.1
  26.7 32.7 %all_gather.3 = bf16[256,2,256]{2,1,0:T(2,128)(2,1)S(1)} all-gather(bf16[32,2,256]{2,1,0:T(2,128)(2,1)S(1)} %copy-done.1), channel_id=1, replica_groups=mesh['row'=64,'col'=8] {'col'}, dimensions={0}, use_global_device_ids=true | all-gather | bytes 294912 | tf_op jit(solution)/shard_map/all_gather | solution.py:8
  59.4 13.5 %all-to-all-done = bf16[64,32,2,256]{3,1,2,0:T(8,128)(2,1)S(1)} async-done(((bf16[64,32,2,256]{3,1,2,0:T(8,128)(2,1)}), bf16[64,32,2,256]{3,1,2,0:T(8,128)(2,1)S(1)}, u32[]{:S(2)}, u32[]{:S(2)}) %all-to-all-start) | async-done | bytes 2097184 | tf_op jit(solution)/shard_map/all_to_all | solution.py:12
  72.9 1.5 copy.10
  74.4 4.1 fusion.1
  78.6 34.7 %all-reduce.1 = bf16[256,2,256]{2,0,1:T(8,128)(2,1)S(1)} all-reduce(f32[256,2,256]{2,0,1:T(8,128)S(1)} %fusion.1), channel_id=1, replica_groups=mesh['row'=64,'col'=8] {'col'}, use_global_device_ids=true, to_apply=%region_0.0 | all-reduce | flops 131072 | bytes 786432 | tf_op jit(solution)/shard_map/psum | solution.py:22
  113.3 0.1 copy.12
  113.4 0.0 copy-done
  113.4 2.7 convolution_bitcast_fusion
  116.1 5.3 %copy.14 = f32[2048,512]{1,0:T(8,128)} copy(f32[2048,512]{0,1:T(8,128)} %convolution_bitcast_fusion) | data formatting | bytes 8388608
  121.5 0.0 reduce-scatter.4.cloned.1.call-update
  121.5 325.6 %reduce-scatter.4.cloned.1.call-done = f32[32,512]{1,0:T(8,128)} async-done(((f32[2048,512]{1,0:T(8,128)}), f32[32,512]{1,0:T(8,128)}) %reduce-scatter.4.cloned.1.call-update) | async-done | bytes 65552
  447.1 1.0 copy.15
  448.0 0.7 copy.13
Async XLA Ops:
  6.5 106.9 %copy-start = (bf16[256,2048]{1,0:T(8,128)(2,1)S(1)}, bf16[256,2048]{1,0:T(8,128)(2,1)}, u32[]{:S(2)}) copy-start(bf16[256,2048]{1,0:T(8,128)(2,1)} %param.5) | copy-start | bytes 3145732
  9.0 64.0 %all-to-all-start = ((bf16[64,32,2,256]{3,1,2,0:T(8,128)(2,1)}), bf16[64,32,2,256]{3,1,2,0:T(8,128)(2,1)S(1)}, u32[]{:S(2)}, u32[]{:S(2)}) async-start(bf16[64,32,2,256]{3,1,2,0:T(8,128)(2,1)} %stack.2), calls=%async_computation | async-start | bytes 4194304 | tf_op jit(solution)/shard_map/all_to_all | solution.py:12
  23.9 2.9 copy-start.1
  23.9 423.2 %reduce-scatter.4.cloned.1.call-start = ((), (), s32[]{:S(2)}) async-start(), calls=%async_computation.2 | async-start | bytes 4259840
Sparse Core Ops, SparseCore 0:
  121.6 325.3 reduce-scatter.3
